TPU v7x, 32 devices: a whole 2x2x4 slice. The times are simulated.
32 devices in a mesh: row: 8 (over z, x), col: 2 (over y), snode: 2 (over core).
Axes of the slice: x: 2, y: 2, z: 4, core: 2. Of those that a mesh axis runs over, the one named last changes fastest.
Arguments:
- ancestor_inverse: bfloat16 [40960, 20480], P(('snode', 'row'), 'col'), parts along dimension 0, may hold values from -8 to 8
- fill_mask: int32 [160, 80], P('snode'), parts along dimension 0, may hold values from 0 to 1, as said below
- block_order: int32 [4, 80], P('snode'), parts along dimension 0, may hold values from 0 to 79, each once within a row
- l_rows: bfloat16 [4, 20480, 256], P('snode', ('row', 'col')), parts along dimension 0, may hold values from -6 to 6
- diag_inverse: bfloat16 [4, 256, 256], P('snode'), parts along dimension 0, may hold values from -0.0024414062 to 0.0024414062
Outputs:
- ainv_kr: bfloat16 [4, 256, 20480], P('snode', None, ('row', 'col')), parts along dimension 0
There are 2 independent parts, one for each index of `snode`. A program takes and returns all parts, laid end to end along the dimension named above; each array names one. Nothing has to cross between parts.
Inputs may be any that keep to these rules, and one draw needn't show every extreme that they name: Tile (i, j) takes part exactly where fill_mask is 1; diagonal tiles are always 1. `block_order`: each row is a permutation of the 80 ancestor blocks.
All inputs are finite; a program needn't handle non-finite values.
Results may differ from a plain program's by a relative error of at most 0.014.
Values may be sent and summed in bfloat16 or wider, within the bound.
A program may use at most 256 MiB of HBM per device.

v0:
```python
import jax
import jax.numpy as jnp
from jax import lax
from jax.sharding import PartitionSpec as P


def per_device(ancestor_inverse, fill_mask, block_order, l_rows, diag_inverse):
    row_index = lax.axis_index("row")
    col_index = lax.axis_index("col")
    local_rows = ancestor_inverse.shape[0]
    local_cols = ancestor_inverse.shape[1]
    snode_count = diag_inverse.shape[0]
    tile_size = diag_inverse.shape[1]
    block_count = fill_mask.shape[0]
    row_blocks = local_rows // tile_size
    col_blocks = local_cols // tile_size
    normed = jnp.einsum(
        "sxy,syz->sxz", l_rows, diag_inverse, preferred_element_type=jnp.float32
    ).astype(jnp.bfloat16)
    wanted = col_index * col_blocks + jnp.arange(col_blocks, dtype=jnp.int32)
    everything = lax.all_gather(normed, ("row", "col"), axis=1, tiled=True)
    pieces = everything.reshape(snode_count, block_count, tile_size, tile_size)
    selector = (block_order[:, None, :] == wanted[None, :, None]).astype(jnp.bfloat16)
    columns = jnp.einsum(
        "saq,sqxy->saxy", selector, pieces, preferred_element_type=jnp.float32
    ).astype(jnp.bfloat16)
    stacked = columns.transpose(1, 2, 0, 3).reshape(local_cols, snode_count * tile_size)
    tile_gate = lax.dynamic_slice(
        fill_mask, (row_index * row_blocks, col_index * col_blocks), (row_blocks, col_blocks)
    ).astype(jnp.bfloat16)
    masked = (
        ancestor_inverse.reshape(row_blocks, tile_size, col_blocks, tile_size)
        * tile_gate[:, None, :, None]
    ).reshape(local_rows, local_cols)
    share_rows = local_rows // lax.axis_size("col")
    own_rows = lax.psum_scatter(
        (-jnp.dot(masked, stacked, preferred_element_type=jnp.float32)).astype(jnp.bfloat16),
        "col",
        scatter_dimension=0,
        tiled=True,
    ).astype(jnp.float32)
    return (
        own_rows.reshape(share_rows, snode_count, tile_size).transpose(1, 2, 0).astype(jnp.bfloat16)
    )


def solution(mesh):
    return jax.shard_map(
        per_device,
        mesh=mesh,
        in_specs=(
            P(("snode", "row"), "col"),
            P("snode", None),
            P("snode", None),
            P("snode", ("row", "col"), None),
            P("snode", None, None),
        ),
        out_specs=P("snode", None, ("row", "col")),
        check_vma=False,
    )
```

profile of v0, /device:TPU:0, one launch (start us, length us, event | category | flops | bytes accessed | tf_op | source)
XLA Modules:
  0.0 385.9 jit_solution(12664486941815667476)
XLA Ops:
  6.5 0.0 copy-start
  6.5 0.0 all-gather.2.cloned.1.call-start
  6.5 1.3 copy-done
  7.9 2.5 convolution_convert_fusion
  10.4 0.0 all-gather.2.cloned.1.call-update
  10.4 0.0 reduce-scatter.2.cloned.1.call-start
  10.4 0.8 dynamic-slice_convert_fusion
  11.2 17.5 %mul.20 = bf16[10,256,40,256]{3,2,1,0:T(8,128)(2,1)} broadcast(bf16[10,40]{1,0:T(8,128)(2,1)S(1)} %dynamic-slice_convert_fusion), dimensions={0,2} | broadcast | bytes 52429600 | tf_op jit(solution)/shard_map/mul | solution.py:32
  28.8 0.0 copy-start.2
  28.8 36.0 %copy.13 = bf16[320,8,40,256]{3,1,2,0:T(8,128)(2,1)} copy(bf16[320,8,40,256]{3,2,1,0:T(8,128)(2,1)} %bitcast.22) | data formatting | bytes 104857600
  64.8 179.1 %all-gather.2.cloned.1.call-done = bf16[2,20480,256]{2,1,0:T(8,128)(2,1)} async-done(((bf16[2,1280,256]{2,1,0:T(8,128)(2,1)}), bf16[2,20480,256]{2,1,0:T(8,128)(2,1)}) %all-gather.2.cloned.1.call-update) | async-done | bytes 20971536 | tf_op jit(solution)/shard_map/all_gather | solution.py:21
  243.9 0.0 copy-done.2
  243.9 25.2 %convert_bitcast_fusion = bf16[40,256,2,256]{3,0,1,2:T(8,128)(2,1)} fusion(bf16[2,80,256,256]{3,2,1,0:T(8,128)(2,1)} %bitcast.25, s32[2,80]{1,0:T(2,128)S(1)} %copy-done.2, s32[40]{0:T(128)S(1)} %iota_add_fusion), kind=kOutput, calls=%fused_computation.4 | convolution fusion | flops 844110080 | bytes 31458080 | tf_op jit(solution)/shard_map/saq,sqxy->saxy/dot_general | solution.py:24
  269.1 17.4 %copy.9 = bf16[40,256,2,256]{1,0,3,2:T(8,128)(2,1)} copy(bf16[40,256,2,256]{3,0,1,2:T(8,128)(2,1)} %convert_bitcast_fusion) | data formatting | bytes 20971520 | tf_op jit(solution)/shard_map/convert_element_type | solution.py:26
  286.5 11.4 %copy.14 = bf16[64,8,40,256]{3,1,2,0:T(8,128)(2,1)} copy(bf16[64,8,40,256]{3,2,1,0:T(8,128)(2,1)} %bitcast.24) | data formatting | bytes 20971520
  297.9 0.0 copy-start.1
  297.9 42.7 %negate_convert_fusion = bf16[2560,512]{1,0:T(8,128)(2,1)} fusion(bf16[10240,512]{0,1:T(8,128)(2,1)} %bitcast.26, bf16[2560,10240]{1,0:T(8,128)(2,1)} %param.5, bf16[2560,10240]{1,0:T(8,128)(2,1)} %bitcast.23), kind=kOutput, calls=%fused_computation.5 | convolution fusion | flops 26872381440 | bytes 117964800 | tf_op jit(solution)/shard_map/dot_general | solution.py:37
  340.6 0.0 reduce-scatter.2.cloned.1.call-update
  340.6 36.0 %reduce-scatter.2.cloned.1.call-done = bf16[1280,512]{1,0:T(8,128)(2,1)} async-done(((bf16[2560,512]{1,0:T(8,128)(2,1)}), bf16[1280,512]{1,0:T(8,128)(2,1)}) %reduce-scatter.2.cloned.1.call-update) | async-done | bytes 1310736 | tf_op jit(solution)/shard_map/reduce_scatter | solution.py:36
  376.6 2.4 copy.12
  379.1 0.0 copy-done.1
  (1 shorter events, 0.0 us)
Async XLA Ops:
  6.5 1.3 copy-start
  6.5 237.4 %all-gather.2.cloned.1.call-start = ((), (), s32[]{:S(2)}) async-start(), calls=%async_computation.1 | async-start | bytes 22282240 | tf_op jit(solution)/shard_map/all_gather | solution.py:21
  10.4 366.3 %reduce-scatter.2.cloned.1.call-start = ((), (), s32[]{:S(2)}) async-start(), calls=%async_computation.2 | async-start | bytes 3932160 | tf_op jit(solution)/shard_map/reduce_scatter | solution.py:36
  28.8 215.2 %copy-start.2 = (s32[2,80]{1,0:T(2,128)S(1)}, s32[2,80]{1,0:T(2,128)}, u32[]{:S(2)}) copy-start(s32[2,80]{1,0:T(2,128)} %param.7) | copy-start | bytes 1924
  297.9 81.1 %copy-start.1 = (bf16[2,1280,256]{2,1,0:T(8,128)(2,1)S(1)}, bf16[2,1280,256]{2,1,0:T(8,128)(2,1)}, u32[]{:S(2)}) copy-start(bf16[2,1280,256]{2,1,0:T(8,128)(2,1)} %param.8) | copy-start | bytes 3932164
Sparse Core Ops, SparseCore 0:
  10.5 233.3 all-gather.1
  340.8 35.8 reduce-scatter.1
where the time goes:
time: 387 us; the launch traced here: 386 us
  waiting for transfers between devices  215 us (56%)
  local copies, waits for them, and re-layouts  86.1 us (22%)
  matrix products  70.4 us (18%)
  between operations  13.4 us (3%)
    all_gather x1, waiting for transfers between devices, per_device(): everything = lax.all_gather(normed, ('row', 'col'), axis=1, tiled=True)  179 us
    unnamed x8, local copies, waits for them, and re-layouts  48.8 us
    dot_general x1, matrix products, per_device(): jnp.dot(masked, stacked, preferred_element_type=jnp.float32)  42.7 us
    reduce_scatter x1, waiting for transfers between devices, per_device(): lax.psum_scatter((-jnp.dot(masked, stacked, preferred_element_type=jnp.fl...  36 us
    dot_general x1, matrix products, per_device(): jnp.einsum('saq,sqxy->saxy', selector, pieces, preferred_element_type=jnp...  25.2 us
    mul x1, local copies, waits for them, and re-layouts, per_device(): ancestor_inverse.reshape(row_blocks, tile_size, col_blocks, tile_size)  17.5 us
    convert_element_type x1, local copies, waits for them, and re-layouts, per_device(): columns = jnp.einsum('saq,sqxy->saxy', selector, pieces, preferred_elemen...  17.4 us
  transfers between devices with their start and end apart: 2, of which 2 were waited for; matrix products, arithmetic and copies ran while one was open for 14% of the time, Pallas kernels for 0%

commit v1 on v0

--- a/solution.py
+++ b/solution.py
@@ -1,16 +1,332 @@
+import functools
+
 import jax
 import jax.numpy as jnp
 from jax import lax
+from jax.experimental import pallas as pl
+from jax.experimental.pallas import tpu as pltpu
 from jax.sharding import PartitionSpec as P
 
-
-def per_device(ancestor_inverse, fill_mask, block_order, l_rows, diag_inverse):
+MESH = pl.DeviceIdType.MESH
+UP, DOWN, XP, YP = range(4)
+
+
+def gather_plan(blocks):
+    fifth = blocks // 5
+    half = max(fifth, 1)
+    plan = []
+    start = 0
+    for order, share in (("zxy", 2 * fifth), ("zyx", 2 * fifth), ("xyz", fifth // 2)):
+        while share > 0:
+            size = min(half, share)
+            plan.append((start, size, order))
+            start += size
+            share -= size
+    while start < blocks:
+        size = min(half, blocks - start)
+        size = min(size, max(fifth // 2, 1))
+        plan.append((start, size, "yxz"))
+        start += size
+    rank = {"zxy": 0, "zyx": 1, "xyz": 2, "yxz": 3}
+    count = {}
+    keyed = []
+    for piece in plan:
+        n = count.get(piece[2], 0)
+        count[piece[2]] = n + 1
+        keyed.append((n, rank[piece[2]], piece))
+    return [piece for _, _, piece in sorted(keyed)]
+
+
+def gather_kernel(depth, plan, own_ref, out_ref, send_sem, recv_sem, local_sem):
+    row = lax.axis_index("row")
+    y = lax.axis_index("col")
+    core = lax.axis_index("snode")
+    z = row // 2
+    x = row % 2
+    where = {
+        UP: ((z + 1) * 2 + x, y, core),
+        DOWN: ((z - 1) * 2 + x, y, core),
+        XP: (z * 2 + 1 - x, y, core),
+        YP: (row, 1 - y, core),
+    }
+    exists = {UP: z + 1 < depth, DOWN: z >= 1}
+
+    barrier = pltpu.get_barrier_semaphore()
+    for way in (XP, YP):
+        pl.semaphore_signal(barrier, inc=1, device_id=where[way], device_id_type=MESH)
+    for way in (UP, DOWN):
+
+        @pl.when(exists[way])
+        def _():
+            pl.semaphore_signal(barrier, inc=1, device_id=where[way], device_id_type=MESH)
+
+    ends = (depth > 1) + (depth > 2)
+    inner = jnp.logical_and(exists[UP], exists[DOWN])
+
+    @pl.when(inner)
+    def _():
+        pl.semaphore_wait(barrier, 2 + ends)
+
+    @pl.when(jnp.logical_not(inner))
+    def _():
+        pl.semaphore_wait(barrier, 2 + (depth > 1))
+
+    me = row * 2 + y
+
+    def slot_of(zz, xx, yy):
+        return (zz * 2 + xx) * 2 + yy
+
+    sent = []
+
+    def descriptor(number, slot, own, way, target=None):
+        start, size, _ = plan[number]
+        span = pl.ds(start, size)
+        source = own_ref.at[span] if own else out_ref.at[slot, span]
+        return pltpu.make_async_remote_copy(
+            src_ref=source,
+            dst_ref=out_ref.at[slot, span],
+            send_sem=send_sem.at[way, slot, number],
+            recv_sem=recv_sem.at[slot, number],
+            device_id=where[way] if target is None else target,
+            device_id_type=MESH,
+        )
+
+    def guarded(cond, fn):
+        if cond is None:
+            fn()
+        else:
+            pl.when(cond)(fn)
+
+    def both(a, b):
+        if a is None:
+            return b
+        if b is None:
+            return a
+        return jnp.logical_and(a, b)
+
+    def send(number, slot, own, way, cond):
+        cond = both(cond, exists.get(way))
+        guarded(cond, lambda: descriptor(number, slot, own, way).start())
+        sent.append((number, slot, own, way, cond))
+
+    def arrived(number, slot, cond):
+        guarded(cond, lambda: descriptor(number, slot, False, XP).wait_recv())
+
+    local = pltpu.make_async_copy(own_ref, out_ref.at[me], local_sem)
+    local.start()
+
+    partner = {"x": XP, "y": YP}
+
+    def coords(flip_x, flip_y):
+        return (1 - x if flip_x else x), (1 - y if flip_y else y)
+
+    reach = [0]
+    for k in range(1, depth):
+        reach += [-k, k]
+
+    def near(dz):
+        if dz == 0:
+            return None
+        return z + dz >= 0 if dz < 0 else z + dz < depth
+
+    def onward_z(number, slot, own, dz, cond):
+        if dz <= 0:
+            send(number, slot, own, UP, cond)
+        if dz >= 0:
+            send(number, slot, own, DOWN, cond)
+
+    def z_first(number, order, dz, level):
+        first, second = order[1], order[2]
+        flips = {0: "", 1: first, 2: second, 3: "xy"}[level]
+        xx, yy = coords("x" in flips, "y" in flips)
+        slot = slot_of(z + dz, xx, yy)
+        own = level == 0 and dz == 0
+        cond = near(dz)
+        if not own:
+            arrived(number, slot, cond)
+        if level == 0:
+            onward_z(number, slot, own, dz, cond)
+            send(number, slot, own, partner[first], cond)
+            send(number, slot, own, partner[second], cond)
+        elif level == 1:
+            send(number, slot, own, partner[second], cond)
+
+    def z_last(number, order, dz, level):
+        first, second = order[0], order[1]
+        flips = {0: "", 1: first, 2: second, 3: "xy"}[level]
+        xx, yy = coords("x" in flips, "y" in flips)
+        slot = slot_of(z + dz, xx, yy)
+        own = level == 0 and dz == 0
+        cond = near(dz)
+        if not own:
+            arrived(number, slot, cond)
+        onward_z(number, slot, own, dz, cond)
+        if dz == 0:
+            if level == 0:
+                send(number, slot, own, partner[first], cond)
+            if level in (0, 1):
+                send(number, slot, own, partner[second], cond)
+
+    def handle(number, dz, level):
+        order = plan[number][2]
+        (z_first if order[0] == "z" else z_last)(number, order, dz, level)
+
+    numbers = range(len(plan))
+    events = []
+    for number in numbers:
+        for position, dz in enumerate(reach):
+            hop = (position + 1) // 2
+            for level in range(4):
+                events.append((2 * hop + (0, 1, 1, 2)[level], number, position, level, dz))
+    events.sort(key=lambda e: e[:4])
+    for _, number, _, level, dz in events:
+        handle(number, dz, level)
+    for number, slot, own, way, cond in sent:
+        guarded(cond, lambda: descriptor(number, slot, own, way).wait_send())
+    local.wait()
+
+
+def gather(own, row_size, col_size):
+    depth = row_size // 2
+    blocks = own.shape[0]
+    plan = gather_plan(blocks)
+    devices = row_size * col_size
+    return pl.pallas_call(
+        functools.partial(gather_kernel, depth, plan),
+        out_shape=jax.ShapeDtypeStruct((devices,) + own.shape, own.dtype),
+        in_specs=[pl.BlockSpec(memory_space=pl.ANY)],
+        out_specs=pl.BlockSpec(memory_space=pl.ANY),
+        scratch_shapes=[
+            pltpu.SemaphoreType.DMA((4, devices, len(plan))),
+            pltpu.SemaphoreType.DMA((devices, len(plan))),
+            pltpu.SemaphoreType.DMA,
+        ],
+        compiler_params=pltpu.CompilerParams(collective_id=0, has_side_effects=True),
+        name="gather",
+    )(own)
+
+
+def product_kernel(snodes, width, tile, table_ref, gate_ref, half_ref, a_ref, *rest):
+    piece_refs = rest[: snodes * width]
+    out_ref, stack_ref, total_ref = rest[snodes * width :]
+    step = pl.program_id(0)
+    for b in range(width):
+        for s in range(snodes):
+            stack_ref[b * tile : (b + 1) * tile, s * tile : (s + 1) * tile] = piece_refs[
+                b * snodes + s
+            ][...]
+
+    @pl.when(step == 0)
+    def _():
+        total_ref[...] = jnp.zeros_like(total_ref)
+
+    row_tiles = a_ref.shape[0] // tile
+    for i in range(row_tiles):
+        rows = slice(i * tile, (i + 1) * tile)
+        parts = []
+        for b in range(width):
+            gate = gate_ref[half_ref[0] * row_tiles + i, step * width + b]
+            part = a_ref[rows, b * tile : (b + 1) * tile]
+            parts.append(part * gate.astype(jnp.float32).astype(part.dtype))
+        total_ref[rows, :] += jnp.dot(
+            jnp.concatenate(parts, axis=1), stack_ref[...], preferred_element_type=jnp.float32
+        )
+
+    @pl.when(step == pl.num_programs(0) - 1)
+    def _():
+        for i in range(row_tiles):
+            rows = slice(i * tile, (i + 1) * tile)
+            out_ref[:, rows] = (-total_ref[rows, :]).T.astype(out_ref.dtype)
+
+
+def product(table, gate, half, ancestor_inverse, pieces, shares, snodes, tile, dtype):
+    local_rows, local_cols = ancestor_inverse.shape
+    rows = local_rows // shares
+    col_blocks = local_cols // tile
+    width = max(w for w in range(1, 6) if col_blocks % w == 0)
+
+    def piece_spec(b, s):
+        return pl.BlockSpec(
+            (pl.Squeezed(), tile, tile),
+            lambda k, table_ref, gate_ref, half_ref: (table_ref[s, k * width + b], 0, 0),
+        )
+
+    return pl.pallas_call(
+        functools.partial(product_kernel, snodes, width, tile),
+        out_shape=jax.ShapeDtypeStruct((snodes * tile, rows), dtype),
+        grid_spec=pltpu.PrefetchScalarGridSpec(
+            num_scalar_prefetch=3,
+            grid=(col_blocks // width,),
+            in_specs=[
+                pl.BlockSpec((rows, width * tile), lambda k, t, g, half_ref: (half_ref[0], k))
+            ]
+            + [piece_spec(b, s) for b in range(width) for s in range(snodes)],
+            out_specs=pl.BlockSpec((snodes * tile, rows), lambda k, t, g, h: (0, 0)),
+            scratch_shapes=[
+                pltpu.VMEM((width * tile, snodes * tile), jnp.bfloat16),
+                pltpu.VMEM((rows, snodes * tile), jnp.float32),
+            ],
+        ),
+        compiler_params=pltpu.CompilerParams(
+            dimension_semantics=("arbitrary",), vmem_limit_bytes=56 * 1024 * 1024
+        ),
+        cost_estimate=pl.CostEstimate(
+            flops=2 * rows * local_cols * snodes * tile,
+            bytes_accessed=2 * rows * local_cols,
+            transcendentals=0,
+        ),
+        name="product",
+    )(table, gate, half, ancestor_inverse, *([pieces] * (snodes * width)))
+
+
+def fast(ancestor_inverse, fill_mask, block_order, l_rows, diag_inverse):
     row_index = lax.axis_index("row")
     col_index = lax.axis_index("col")
-    local_rows = ancestor_inverse.shape[0]
-    local_cols = ancestor_inverse.shape[1]
-    snode_count = diag_inverse.shape[0]
-    tile_size = diag_inverse.shape[1]
+    row_size = lax.axis_size("row")
+    col_size = lax.axis_size("col")
+    local_rows, local_cols = ancestor_inverse.shape
+    snodes, tile = diag_inverse.shape[:2]
+    row_blocks = local_rows // tile
+    col_blocks = local_cols // tile
+    held = l_rows.shape[1] // tile
+    normed = jnp.einsum(
+        "sxy,syz->sxz", l_rows, diag_inverse, preferred_element_type=jnp.float32
+    ).astype(jnp.bfloat16)
+    own = normed.reshape(snodes * held, tile, tile)
+    pieces = gather(own, row_size, col_size).reshape(-1, tile, tile)
+
+    wanted = col_index * col_blocks + jnp.arange(col_blocks, dtype=jnp.int32)
+    packed = jnp.arange(block_order.shape[1], dtype=jnp.int32)
+    place = jnp.sum(
+        jnp.where(block_order[:, None, :] == wanted[None, :, None], packed[None, None, :], 0), axis=2
+    )
+    table = (
+        (place // held) * (snodes * held)
+        + jnp.arange(snodes, dtype=jnp.int32)[:, None] * held
+        + place % held
+    ).astype(jnp.int32)
+    gate = lax.dynamic_slice(
+        fill_mask, (row_index * row_blocks, col_index * col_blocks), (row_blocks, col_blocks)
+    )
+
+    def share(half, dtype):
+        return product(
+            table, gate, half.reshape(1).astype(jnp.int32), ancestor_inverse, pieces,
+            col_size, snodes, tile, dtype,
+        )
+
+    theirs = share(1 - col_index, jnp.bfloat16)
+    received = lax.ppermute(theirs, "col", [(0, 1), (1, 0)])
+    mine = share(col_index, jnp.float32)
+    total = (mine + received.astype(jnp.float32)).astype(jnp.bfloat16)
+    return total.reshape(snodes, tile, local_rows // col_size)
+
+
+def plain(ancestor_inverse, fill_mask, block_order, l_rows, diag_inverse):
+    row_index = lax.axis_index("row")
+    col_index = lax.axis_index("col")
+    local_rows, local_cols = ancestor_inverse.shape
+    snode_count, tile_size = diag_inverse.shape[:2]
     block_count = fill_mask.shape[0]
     row_blocks = local_rows // tile_size
     col_blocks = local_cols // tile_size
@@ -44,6 +360,19 @@
     )
 
 
+def per_device(ancestor_inverse, fill_mask, block_order, l_rows, diag_inverse):
+    tile = diag_inverse.shape[1]
+    col_size = lax.axis_size("col")
+    if (
+        col_size == 2
+        and lax.axis_size("row") % 2 == 0
+        and l_rows.shape[1] % tile == 0
+        and ancestor_inverse.shape[0] % (col_size * tile) == 0
+    ):
+        return fast(ancestor_inverse, fill_mask, block_order, l_rows, diag_inverse)
+    return plain(ancestor_inverse, fill_mask, block_order, l_rows, diag_inverse)
+
+
 def solution(mesh):
     return jax.shard_map(
         per_device,

time: 387 us -> 223 us (0.58)
  waiting for transfers between devices: 215 us -> 4.1 us
  Pallas kernels: 0 us -> 209 us
  local copies, waits for them, and re-layouts: 86.1 us -> 2.69 us
  matrix products: 70.4 us -> 2.5 us
  between operations: 13.4 us -> 0.02 us
    pallas_call x0 -> x3, Pallas kernels: none -> 209 us  [the longest x1 164 us: gather(): pl.pallas_call(functools.partial(gather_kernel, depth, plan), out_shape=j...]
    all_gather x1 -> x0, waiting for transfers between devices: 179 us -> none  [per_device(): everything = lax.all_gather(normed, ('row', 'col'), axis=1, tiled=True)]
    dot_general x3 -> x1, matrix products: 70.4 us -> 2.5 us  [fast(): jnp.einsum('sxy,syz->sxz', l_rows, diag_inverse, preferred_element_type=j...]
    unnamed x8 -> x6, local copies, waits for them, and re-layouts: 48.8 us -> 1.32 us
    reduce_scatter x1 -> x0, waiting for transfers between devices: 36 us -> none  [per_device(): lax.psum_scatter((-jnp.dot(masked, stacked, preferred_element_type=jnp.fl...]
    convert_element_type x2 -> x0, local copies, waits for them, and re-layouts: 19.8 us -> none  [the longest x1 17.4 us: per_device(): columns = jnp.einsum('saq,sqxy->saxy', selector, pieces, preferred_elemen...]
    mul x1 -> x0, local copies, waits for them, and re-layouts: 17.5 us -> none  [per_device(): ancestor_inverse.reshape(row_blocks, tile_size, col_blocks, tile_size)]
    ppermute x0 -> x1, waiting for transfers between devices: none -> 4.1 us  [fast(): received = lax.ppermute(theirs, 'col', [(0, 1), (1, 0)])]
  transfers between devices with their start and end apart: 2 -> 1, of which waited for: 2 -> 1; matrix products, arithmetic and copies ran while one was open for 14% -> 0% of each run, Pallas kernels for 0% -> 10%
where the time goes in v1:
time: 223 us
  Pallas kernels  209 us (94%)
  waiting for transfers between devices  4.1 us (2%)
  other arithmetic  3.98 us (2%)
  local copies, waits for them, and re-layouts  2.69 us (1%)
  matrix products  2.5 us (1%)
    pallas_call x1, Pallas kernels, gather(): pl.pallas_call(functools.partial(gather_kernel, depth, plan), out_shape=j...  164 us
    pallas_call x2, Pallas kernels, product(): pl.pallas_call(functools.partial(product_kernel, snodes, width, tile), ou...  45.1 us
  transfers between devices with their start and end apart: 1, of which 1 were waited for; matrix products, arithmetic and copies ran while one was open for 0% of the time, Pallas kernels for 10%

profile of v1, /device:TPU:0, one launch (start us, length us, event | category | flops | bytes accessed | tf_op | source)
XLA Modules:
  0.0 222.8 jit_solution(4562951634280299089)
XLA Ops:
  0.0 0.0 copy-start
  0.0 1.3 copy-done
  1.3 2.5 %convolution_convert_fusion = bf16[2,1280,256]{2,1,0:T(8,128)(2,1)} fusion(bf16[2,1280,256]{2,1,0:T(8,128)(2,1)S(1)} %copy-done, bf16[2,256,256]{2,1,0:T(8,128)(2,1)} %param.9), kind=kOutput, calls=%fused_computation | convolution fusion | flops 336199680 | bytes 2883584 | tf_op jit(solution)/shard_map/sxy,syz->sxz/dot_general | solution.py:292
  3.8 0.0 copy-start.2
  3.8 163.8 %gather.1 = bf16[16,10,256,256]{3,2,1,0:T(8,128)(2,1)} custom-call(bf16[10,256,256]{2,1,0:T(8,128)(2,1)} %bitcast.27), custom_call_target="tpu_custom_call" | custom-call | tf_op jit(solution)/shard_map/gather/pallas_call | solution.py:194
  167.7 0.0 copy-done.2
  167.7 0.2 select_reduce_fusion
  167.8 0.6 fusion.table_ref
  168.5 1.4 dynamic_slice.3.gate_ref
  169.9 22.2 %product.3 = bf16[512,1280]{1,0:T(8,128)(2,1)} custom-call(s32[2,40]{1,0:T(2,128)} %fusion.table_ref, s32[10,40]{1,0:T(8,128)} %dynamic_slice.3.gate_ref, s32[1]{0:T(128)} %bitcast.3.half_ref, bf16[2560,10240]{1,0:T(8,128)(2,1)} %a_ref.3, bf16[160,256,256]{2,1,0:T(8,128)(2,1)} %bitcast.7, bf16[160,256,256]{2,1,0:T(8,128)(2,1)} %bitcast.8, ...), custom_call_target="tpu_custom_call" | custom-call | flops 13421772800 | bytes 26214400 | tf_op jit(solution)/shard_map/product/pallas_call | solution.py:254
  192.1 0.5 collective-permute-start
  192.6 22.9 %product.2 = f32[512,1280]{1,0:T(8,128)} custom-call(s32[2,40]{1,0:T(2,128)} %fusion.table_ref, s32[10,40]{1,0:T(8,128)} %dynamic_slice.3.gate_ref, s32[1]{0:T(128)} %bitcast.half_ref, bf16[2560,10240]{1,0:T(8,128)(2,1)} %a_ref.3, bf16[160,256,256]{2,1,0:T(8,128)(2,1)} %bitcast.17, bf16[160,256,256]{2,1,0:T(8,128)(2,1)} %bitcast.18, ...), custom_call_target="tpu_custom_call" | custom-call | flops 13421772800 | bytes 26214400 | tf_op jit(solution)/shard_map/product/pallas_call | solution.py:254
  215.5 4.1 %collective-permute-done = bf16[512,1280]{1,0:T(8,128)(2,1)S(1)} collective-permute-done((bf16[512,1280]{1,0:T(8,128)(2,1)}, bf16[512,1280]{1,0:T(8,128)(2,1)S(1)}, u32[]{:S(2)}, u32[]{:S(2)}) %collective-permute-start) | collective-permute-done | bytes 1310752 | tf_op jit(solution)/shard_map/ppermute | solution.py:319
  219.6 0.0 copy-start.1
  219.6 3.2 %add_convert_fusion = bf16[512,1280]{1,0:T(8,128)(2,1)} fusion(f32[512,1280]{1,0:T(8,128)} %product.2, bf16[512,1280]{1,0:T(8,128)(2,1)S(1)} %collective-permute-done), kind=kLoop, calls=%fused_computation.1 | loop fusion | flops 1966080 | bytes 5242880 | tf_op jit(solution)/shard_map/convert_element_type | solution.py:321
  222.8 0.0 copy-done.1
  (2 shorter events, 0.0 us)
Async XLA Ops:
  0.0 1.3 copy-start
  3.8 163.8 %copy-start.2 = (s32[2,80]{1,0:T(2,128)S(1)}, s32[2,80]{1,0:T(2,128)}, u32[]{:S(2)}) copy-start(s32[2,80]{1,0:T(2,128)} %param.7) | copy-start | bytes 1924
  192.1 27.6 %collective-permute-start = (bf16[512,1280]{1,0:T(8,128)(2,1)}, bf16[512,1280]{1,0:T(8,128)(2,1)S(1)}, u32[]{:S(2)}, u32[]{:S(2)}) collective-permute-start(bf16[512,1280]{1,0:T(8,128)(2,1)} %product.3), channel_id=1, source_target_pairs={{0,2},{2,0},{1,3},{3,1},{4,6},{6,4},{5,7},{7,5},{8,10},{10,8},{9,1... | collective-permute-start | bytes 3932168 | tf_op jit(solution)/shard_map/ppermute | solution.py:319
  219.6 3.2 %copy-start.1 = (bf16[2,1280,256]{2,1,0:T(8,128)(2,1)S(1)}, bf16[2,1280,256]{2,1,0:T(8,128)(2,1)}, u32[]{:S(2)}) copy-start(bf16[2,1280,256]{2,1,0:T(8,128)(2,1)} %param.8) | copy-start | bytes 3932164

commit v2 on v1

--- a/solution.py
+++ b/solution.py
@@ -177,7 +177,7 @@
         for position, dz in enumerate(reach):
             hop = (position + 1) // 2
             for level in range(4):
-                events.append((2 * hop + (0, 1, 1, 2)[level], number, position, level, dz))
+                events.append((2 * hop + (0, 2, 2, 4)[level], number, position, level, dz))
     events.sort(key=lambda e: e[:4])
     for _, number, _, level, dz in events:
         handle(number, dz, level)

time: 223 us -> 215 us (0.964)
  Pallas kernels: 209 us -> 200 us
    pallas_call x1, Pallas kernels: 164 us -> 155 us  [gather(): pl.pallas_call(functools.partial(gather_kernel, depth, plan), out_shape=j...]
  transfers between devices with their start and end apart: 1 -> 1, of which waited for: 1 -> 1; matrix products, arithmetic and copies ran while one was open for 0% -> 0% of each run, Pallas kernels for 10% -> 11%
where the time goes in v2:
time: 215 us; the launch traced here: 214 us
  Pallas kernels  200 us (93%)
  other arithmetic  3.98 us (2%)
  waiting for transfers between devices  3.71 us (2%)
  local copies, waits for them, and re-layouts  2.69 us (1%)
  matrix products  2.5 us (1%)
    pallas_call x1, Pallas kernels, gather(): pl.pallas_call(functools.partial(gather_kernel, depth, plan), out_shape=j...  155 us
    pallas_call x2, Pallas kernels, product(): pl.pallas_call(functools.partial(product_kernel, snodes, width, tile), ou...  45.2 us
  transfers between devices with their start and end apart: 1, of which 1 were waited for; matrix products, arithmetic and copies ran while one was open for 0% of the time, Pallas kernels for 11%

profile of v2, /device:TPU:0, one launch (start us, length us, event | category | flops | bytes accessed | tf_op | source)
XLA Modules:
  0.0 214.5 jit_solution(4937137395382960231)
XLA Ops:
  0.0 0.0 copy-start
  0.0 1.3 copy-done
  1.3 2.5 %convolution_convert_fusion = bf16[2,1280,256]{2,1,0:T(8,128)(2,1)} fusion(bf16[2,1280,256]{2,1,0:T(8,128)(2,1)S(1)} %copy-done, bf16[2,256,256]{2,1,0:T(8,128)(2,1)} %param.9), kind=kOutput, calls=%fused_computation | convolution fusion | flops 336199680 | bytes 2883584 | tf_op jit(solution)/shard_map/sxy,syz->sxz/dot_general | solution.py:292
  3.8 0.0 copy-start.2
  3.8 154.9 %gather.1 = bf16[16,10,256,256]{3,2,1,0:T(8,128)(2,1)} custom-call(bf16[10,256,256]{2,1,0:T(8,128)(2,1)} %bitcast.27), custom_call_target="tpu_custom_call" | custom-call | tf_op jit(solution)/shard_map/gather/pallas_call | solution.py:194
  158.7 0.0 copy-done.2
  158.7 0.2 select_reduce_fusion
  158.9 0.6 fusion.table_ref
  159.6 1.4 dynamic_slice.3.gate_ref
  160.9 22.2 %product.3 = bf16[512,1280]{1,0:T(8,128)(2,1)} custom-call(s32[2,40]{1,0:T(2,128)} %fusion.table_ref, s32[10,40]{1,0:T(8,128)} %dynamic_slice.3.gate_ref, s32[1]{0:T(128)} %bitcast.3.half_ref, bf16[2560,10240]{1,0:T(8,128)(2,1)} %a_ref.3, bf16[160,256,256]{2,1,0:T(8,128)(2,1)} %bitcast.7, bf16[160,256,256]{2,1,0:T(8,128)(2,1)} %bitcast.8, ...), custom_call_target="tpu_custom_call" | custom-call | flops 13421772800 | bytes 26214400 | tf_op jit(solution)/shard_map/product/pallas_call | solution.py:254
  183.1 1.5 collective-permute-start
  184.6 23.0 %product.2 = f32[512,1280]{1,0:T(8,128)} custom-call(s32[2,40]{1,0:T(2,128)} %fusion.table_ref, s32[10,40]{1,0:T(8,128)} %dynamic_slice.3.gate_ref, s32[1]{0:T(128)} %bitcast.half_ref, bf16[2560,10240]{1,0:T(8,128)(2,1)} %a_ref.3, bf16[160,256,256]{2,1,0:T(8,128)(2,1)} %bitcast.17, bf16[160,256,256]{2,1,0:T(8,128)(2,1)} %bitcast.18, ...), custom_call_target="tpu_custom_call" | custom-call | flops 13421772800 | bytes 26214400 | tf_op jit(solution)/shard_map/product/pallas_call | solution.py:254
  207.6 3.7 %collective-permute-done = bf16[512,1280]{1,0:T(8,128)(2,1)S(1)} collective-permute-done((bf16[512,1280]{1,0:T(8,128)(2,1)}, bf16[512,1280]{1,0:T(8,128)(2,1)S(1)}, u32[]{:S(2)}, u32[]{:S(2)}) %collective-permute-start) | collective-permute-done | bytes 1310752 | tf_op jit(solution)/shard_map/ppermute | solution.py:319
  211.3 0.0 copy-start.1
  211.3 3.2 %add_convert_fusion = bf16[512,1280]{1,0:T(8,128)(2,1)} fusion(f32[512,1280]{1,0:T(8,128)} %product.2, bf16[512,1280]{1,0:T(8,128)(2,1)S(1)} %collective-permute-done), kind=kLoop, calls=%fused_computation.1 | loop fusion | flops 1966080 | bytes 5242880 | tf_op jit(solution)/shard_map/convert_element_type | solution.py:321
  214.5 0.0 copy-done.1
  (2 shorter events, 0.0 us)
Async XLA Ops:
  0.0 1.3 copy-start
  3.8 154.9 %copy-start.2 = (s32[2,80]{1,0:T(2,128)S(1)}, s32[2,80]{1,0:T(2,128)}, u32[]{:S(2)}) copy-start(s32[2,80]{1,0:T(2,128)} %param.7) | copy-start | bytes 1924
  183.1 28.2 %collective-permute-start = (bf16[512,1280]{1,0:T(8,128)(2,1)}, bf16[512,1280]{1,0:T(8,128)(2,1)S(1)}, u32[]{:S(2)}, u32[]{:S(2)}) collective-permute-start(bf16[512,1280]{1,0:T(8,128)(2,1)} %product.3), channel_id=1, source_target_pairs={{0,2},{2,0},{1,3},{3,1},{4,6},{6,4},{5,7},{7,5},{8,10},{10,8},{9,1... | collective-permute-start | bytes 3932168 | tf_op jit(solution)/shard_map/ppermute | solution.py:319
  211.3 3.2 %copy-start.1 = (bf16[2,1280,256]{2,1,0:T(8,128)(2,1)S(1)}, bf16[2,1280,256]{2,1,0:T(8,128)(2,1)}, u32[]{:S(2)}) copy-start(bf16[2,1280,256]{2,1,0:T(8,128)(2,1)} %param.8) | copy-start | bytes 3932164
